TPU v7x, 32 devices: a whole 2x2x4 slice. The times are simulated.
32 devices in a mesh: grp: 4 (over y, core), dev: 8 (over z, x).
Axes of the slice: x: 2, y: 2, z: 4, core: 2. Of those that a mesh axis runs over, the one named last changes fastest.
Arguments:
- centers: bfloat16 [4096, 128], P(('grp', 'dev')), may hold values from -4 to 4
- center_weights: bfloat16 [4096, 64], P(('grp', 'dev')), may hold values from -0.75 to 0.75
- batch: bfloat16 [8192, 128], P('dev'), may hold values from -4 to 4
- labels: bfloat16 [8192, 64], P('dev'), may hold values from -6 to 6
- sub_centers: bfloat16 [2048, 128], P('grp'), may hold values from -4 to 4
- eig_vectors: bfloat16 [2048, 160], P('grp'), may hold values from -0.5 to 0.5
- eig_scale: float32 [160], replicated, may hold values from 0.02 to 0.4
Outputs:
- predictions: float32 [8192, 64], P('dev')
- center_step: float32 [4096, 64], P(('grp', 'dev'))
- nystrom_fix: float32 [2048, 64], P('grp')
All inputs are finite; a program needn't handle non-finite values.
Results may differ from a plain program's by a relative error of at most 0.0031.
Values may be sent and summed in bfloat16 or wider, within the bound.
A program may use at most 64 MiB of HBM per device.

v0:
```python
import math
import jax
import jax.numpy as jnp
from jax import lax
from jax.sharding import PartitionSpec as P

gamma_scale = 0.25
learn_rate = 8.0


def sq_norms(points):
    return jnp.sum(jnp.square(points.astype(jnp.float32)), axis=1)


def kernel_tile(left, left_sq, right, right_sq):
    cross = lax.dot_general(
        left, right, (((1,), (1,)), ((), ())), preferred_element_type=jnp.float32
    )
    dist = left_sq[:, None] + right_sq[None, :] - 2.0 * cross
    return jnp.exp(-gamma_scale * dist).astype(jnp.bfloat16)


def body(centers, center_weights, batch, labels, sub_centers, eig_vectors, eig_scale):
    samples = batch.shape[0]
    width_in = batch.shape[1]
    width_out = labels.shape[1]
    block = min(512, samples)
    num_blocks = samples // block
    factor = learn_rate / math.sqrt(samples * lax.axis_size("dev"))
    batch_sq = sq_norms(batch)
    batch_blocks = batch.reshape(num_blocks, block, width_in)
    sq_blocks = batch_sq.reshape(num_blocks, block)
    group_centers, group_weights = (
        lax.all_gather(centers, "dev", axis=0, tiled=True),
        lax.all_gather(center_weights, "dev", axis=0, tiled=True),
    )
    group_sq = sq_norms(group_centers)

    def pred_rows(inputs):
        rows_x, rows_sq = inputs
        tile = kernel_tile(rows_x, rows_sq, group_centers, group_sq)
        return jnp.dot(tile, group_weights, preferred_element_type=jnp.float32)

    partial_pred = lax.map(pred_rows, (batch_blocks, sq_blocks)).reshape(samples, width_out)
    predictions = lax.psum(partial_pred, "grp")
    resid = (predictions - labels.astype(jnp.float32)).astype(jnp.bfloat16)
    resid_blocks = resid.reshape(num_blocks, block, width_out)
    rows_sq = group_sq

    def add_block(accum, inputs):
        rows_x, part_sq, rows_r = inputs
        tile = kernel_tile(group_centers, rows_sq, rows_x, part_sq)
        return (accum + jnp.dot(tile, rows_r, preferred_element_type=jnp.float32), None)

    result, _ = lax.scan(
        add_block,
        jnp.zeros((lax.axis_size("dev") * centers.shape[0], width_out), jnp.float32),
        (batch_blocks, sq_blocks, resid_blocks),
    )
    center_step = lax.psum_scatter(result, "dev", scatter_dimension=0, tiled=True) * factor
    sub_sq = sq_norms(sub_centers)

    def sub_block(accum, inputs):
        rows_x, rows_sq, rows_r = inputs
        tile = kernel_tile(sub_centers, sub_sq, rows_x, rows_sq)
        return (accum + jnp.dot(tile, rows_r, preferred_element_type=jnp.float32), None)

    sub_part, _ = lax.scan(
        sub_block,
        jnp.zeros((sub_centers.shape[0], width_out), jnp.float32),
        (batch_blocks, sq_blocks, resid_blocks),
    )
    sub_part = sub_part * factor
    vectors = eig_vectors.astype(jnp.float32)
    dims = (((0,), (0,)), ((), ()))
    proj_part = lax.dot_general(vectors, sub_part, dims, precision=lax.Precision.HIGHEST)
    proj = lax.psum(proj_part, ("grp", "dev"))
    nystrom_fix = jnp.dot(vectors, eig_scale[:, None] * proj, precision=lax.Precision.HIGHEST)
    return (predictions, center_step, nystrom_fix)


def solution(mesh):
    placed = (
        P(("grp", "dev"), None),
        P(("grp", "dev"), None),
        P("dev", None),
        P("dev", None),
        P("grp", None),
        P("grp", None),
        P(),
    )
    return jax.shard_map(
        body,
        mesh=mesh,
        in_specs=placed,
        out_specs=(P("dev", None), P(("grp", "dev"), None), P("grp", None)),
        check_vma=False,
    )
```

profile of v0, /device:TPU:0, one launch (start us, length us, event | category | flops | bytes accessed | tf_op | source)
XLA Modules:
  0.0 186.0 jit_solution(1019431074230919624)
XLA Ops:
  7.2 32.9 %all_gather.6 = bf16[1024,128]{1,0:T(8,128)(2,1)S(1)} all-gather(bf16[128,128]{1,0:T(8,128)(2,1)} %param.13), channel_id=1, replica_groups=mesh['grp'=4,'dev'=8] {'dev'}, dimensions={0}, use_global_device_ids=true | all-gather | bytes 294912 | tf_op jit(solution)/shard_map/all_gather | solution.py:34
  40.1 0.2 multiply_reduce_fusion
  40.4 0.2 multiply_reduce_fusion.1
  40.6 0.3 copy-done.6
  40.9 0.1 copy.10
  41.0 30.7 %all_gather.7 = bf16[1024,64]{1,0:T(8,128)(2,1)S(1)} all-gather(bf16[128,64]{1,0:T(8,128)(2,1)S(1)} %copy.10), channel_id=1, replica_groups=mesh['grp'=4,'dev'=8] {'dev'}, dimensions={0}, use_global_device_ids=true | all-gather | bytes 147456 | tf_op jit(solution)/shard_map/all_gather | solution.py:35
  71.7 4.5 %while.32 = (s32[]{:T(128)}, f32[2,512,64]{1,0,2:T(2,128)S(1)}, f32[2,512]{1,0:T(2,128)S(1)}, f32[1024]{0:T(1024)S(1)}, bf16[2,512,128]{2,1,0:T(8,128)(2,1)S(1)}...) while((s32[]{:T(128)}, f32[2,512,64]{1,0,2:T(2,128)S(1)}, ...), condition=%wide.region_3.4_spmd, body=%wide.region_2.3_spmd.sunk | while | flops 203948032 | bytes 1321065 | solution.py:44
  71.7 0.9 fusion.81
  72.6 0.1 copy.22
  72.7 1.2 dynamic_update_slice.5
  74.0 0.9 fusion.81
  74.9 0.1 copy.22
  75.0 1.2 dynamic_update_slice.5
  76.2 0.8 copy.20
  77.1 0.8 copy-done.4
  77.9 0.1 multiply_reduce_fusion.2
  78.0 32.6 %all-reduce.2.cloned.1.call-done = f32[1024,64]{0,1:T(8,128)} async-done(((f32[1024,64]{0,1:T(8,128)}), f32[1024,64]{0,1:T(8,128)}) %all-reduce.2.cloned.1.call-update) | async-done | bytes 262160 | tf_op jit(solution)/shard_map/psum | solution.py:45
  110.6 1.0 subtract_convert_fusion
  111.6 0.2 copy.14
  111.8 1.8 while.33
  111.8 0.9 fusion.85
  112.7 0.9 fusion.85
  113.6 0.7 copy-done.3
  114.3 1.3 while.34
  114.3 0.6 fusion.89
  115.0 0.6 fusion.89
  115.6 0.3 convolution_bitcast_fusion.1
  115.9 40.1 %psum.15 = f32[160,64]{1,0:T(8,128)S(1)} all-reduce(f32[160,64]{1,0:T(8,128)S(1)} %convolution_bitcast_fusion.1), channel_id=1, replica_groups=mesh['grp'=4,'dev'=8] {'grp','dev'}, use_global_device_ids=true, to_apply=%region_11.12 | all-reduce | flops 10240 | bytes 81920 | tf_op jit(solution)/shard_map/psum | solution.py:77
  156.0 1.0 convolution_bitcast_fusion
  157.0 20.0 %reduce-scatter.2.cloned.1.call-done = f32[128,64]{0,1:T(8,128)} async-done(((f32[1024,64]{0,1:T(8,128)}), f32[128,64]{0,1:T(8,128)}) %reduce-scatter.2.cloned.1.call-update) | async-done | bytes 32784 | tf_op jit(solution)/shard_map/reduce_scatter | solution.py:60
  177.0 1.4 broadcast_multiply_fusion
  178.4 0.7 copy.43
  (27 shorter events, 0.2 us)
Async XLA Ops:
  7.2 108.4 %copy-start = (bf16[512,160]{0,1:T(8,128)(2,1)S(1)}, bf16[512,160]{0,1:T(8,128)(2,1)}, u32[]{:S(2)}) copy-start(bf16[512,160]{0,1:T(8,128)(2,1)} %param.18) | copy-start | bytes 491524
  7.2 103.4 %all-reduce.2.cloned.1.call-start = ((), (), s32[]{:S(2)}) async-start(), calls=%async_computation.1 | async-start | bytes 524288 | tf_op jit(solution)/shard_map/psum | solution.py:45
  7.2 33.1 %copy-start.2 = (bf16[1024,128]{1,0:T(8,128)(2,1)S(1)}, bf16[1024,128]{1,0:T(8,128)(2,1)}, u32[]{:S(2)}) copy-start(bf16[1024,128]{1,0:T(8,128)(2,1)} %param.15) | copy-start | bytes 786436
  40.1 0.7 copy-start.6
  77.0 0.9 copy-start.4
  77.0 33.6 %copy-start.5 = (bf16[1024,64]{0,1:T(8,128)(2,1)S(1)}, bf16[1024,64]{0,1:T(8,128)(2,1)}, u32[]{:S(2)}) copy-start(bf16[1024,64]{0,1:T(8,128)(2,1)} %param.16) | copy-start | bytes 393220
  77.0 100.0 %reduce-scatter.2.cloned.1.call-start = ((), (), s32[]{:S(2)}) async-start(), calls=%async_computation.2 | async-start | bytes 294912 | tf_op jit(solution)/shard_map/reduce_scatter | solution.py:60
  113.6 0.7 copy-start.3
  115.6 40.4 %copy-start.7 = (f32[160]{0:T(256)S(1)}, f32[160]{0:T(256)}, u32[]{:S(2)}) copy-start(f32[160]{0:T(256)} %param.19) | copy-start | bytes 1924
  156.0 22.4 %copy-start.1 = (f32[1024,64]{0,1:T(8,128)S(1)}, f32[1024,64]{0,1:T(8,128)}, u32[]{:S(2)}) copy-start(f32[1024,64]{0,1:T(8,128)} %all-reduce.2.cloned.1.call-done) | copy-start | bytes 786436
Sparse Core Ops, SparseCore 0:
  77.1 33.4 all-reduce.1
  114.5 62.5 reduce-scatter.1
where the time goes:
time: 186 us
  blocking collectives  104 us (56%)
  waiting for transfers between devices  52.6 us (28%)
  between operations  14.2 us (8%)
  local copies, waits for them, and re-layouts  6.28 us (3%)
  matrix products  5.97 us (3%)
  other arithmetic  2.92 us (2%)
    psum x1, blocking collectives, body(): proj = lax.psum(proj_part, ('grp', 'dev'))  40.1 us
    all_gather x1, blocking collectives, body(): lax.all_gather(centers, 'dev', axis=0, tiled=True)  32.9 us
    psum x1, waiting for transfers between devices, body(): predictions = lax.psum(partial_pred, 'grp')  32.6 us
    all_gather x1, blocking collectives, body(): lax.all_gather(center_weights, 'dev', axis=0, tiled=True)  30.7 us
    reduce_scatter x1, waiting for transfers between devices, body(): lax.psum_scatter(result, 'dev', scatter_dimension=0, tiled=True) * factor  20 us
  transfers between devices with their start and end apart: 2, of which 2 were waited for; matrix products, arithmetic and copies ran while one was open for 1% of the time, Pallas kernels for 0%

commit v1 on v0

--- a/solution.py
+++ b/solution.py
@@ -6,6 +6,17 @@
 
 gamma_scale = 0.25
 learn_rate = 8.0
+
+
+def ring_gather(x, axis, dim):
+    ways = lax.axis_size(axis)
+    pieces = [x]
+    for far in range(1, ways):
+        pieces.append(
+            lax.ppermute(pieces[far - 1], axis, [(d, (d - 1) % ways) for d in range(ways)])
+        )
+    line = jnp.concatenate(pieces, axis=dim)
+    return jnp.roll(line, lax.axis_index(axis) * x.shape[dim], axis=dim)
 
 
 def sq_norms(points):
@@ -32,7 +43,7 @@
     sq_blocks = batch_sq.reshape(num_blocks, block)
     group_centers, group_weights = (
         lax.all_gather(centers, "dev", axis=0, tiled=True),
-        lax.all_gather(center_weights, "dev", axis=0, tiled=True),
+        ring_gather(center_weights, "dev", 0),
     )
     group_sq = sq_norms(group_centers)
 

time: 186 us -> 196 us (1.054)
  blocking collectives: 104 us -> 71 us
  starting transfers between devices: 0.08 us -> 30 us
  waiting for transfers between devices: 52.6 us -> 65.4 us
    all_gather x1 -> x0, blocking collectives: 30.7 us -> none  [body(): lax.all_gather(center_weights, 'dev', axis=0, tiled=True)]
    ppermute x0 -> x7, starting transfers between devices: none -> 29.9 us  [ring_gather(): lax.ppermute(pieces[far - 1], axis, [(d, (d - 1) % ways) for d in range(w...]
    ppermute x0 -> x7, waiting for transfers between devices: none -> 11.5 us  [ring_gather(): lax.ppermute(pieces[far - 1], axis, [(d, (d - 1) % ways) for d in range(w...]
  transfers between devices with their start and end apart: 2 -> 9, of which waited for: 2 -> 8; matrix products, arithmetic and copies ran while one was open for 1% -> 2% of each run, Pallas kernels for 0% -> 0%
where the time goes in v1:
time: 196 us
  blocking collectives  71 us (36%)
  waiting for transfers between devices  65.4 us (33%)
  starting transfers between devices  30 us (15%)
  between operations  14.3 us (7%)
  local copies, waits for them, and re-layouts  6.19 us (3%)
  matrix products  5.98 us (3%)
  other arithmetic  2.92 us (1%)
    psum x1, blocking collectives, body(): proj = lax.psum(proj_part, ('grp', 'dev'))  40.1 us
    psum x1, waiting for transfers between devices, body(): predictions = lax.psum(partial_pred, 'grp')  33.9 us
    all_gather x1, blocking collectives, body(): lax.all_gather(centers, 'dev', axis=0, tiled=True)  31 us
    ppermute x7, starting transfers between devices, ring_gather(): lax.ppermute(pieces[far - 1], axis, [(d, (d - 1) % ways) for d in range(w...  29.9 us
    reduce_scatter x1, waiting for transfers between devices, body(): lax.psum_scatter(result, 'dev', scatter_dimension=0, tiled=True) * factor  20 us
    ppermute x7, waiting for transfers between devices, ring_gather(): lax.ppermute(pieces[far - 1], axis, [(d, (d - 1) % ways) for d in range(w...  11.5 us
  transfers between devices with their start and end apart: 9, of which 8 were waited for; matrix products, arithmetic and copies ran while one was open for 2% of the time, Pallas kernels for 0%

profile of v1, /device:TPU:0, one launch (start us, length us, event | category | flops | bytes accessed | tf_op | source)
XLA Modules:
  0.0 196.0 jit_solution(5597858175779662054)
XLA Ops:
  7.2 0.9 copy.11
  8.1 6.1 %collective-permute-start = (bf16[128,64]{1,0:T(8,128)(2,1)S(1)}, bf16[128,64]{1,0:T(8,128)(2,1)S(1)}, u32[]{:S(2)}, u32[]{:S(2)}) collective-permute-start(bf16[128,64]{1,0:T(8,128)(2,1)S(1)} %copy.11), channel_id=1, source_target_pairs={{0,7},{1,0},{2,1},{3,2},{4,3},{5,4},{6,5},{7,6},{8,15},{9,8},{10,9... | collective-permute-start | bytes 49160 | tf_op jit(solution)/shard_map/ppermute | solution.py:16
  14.2 31.0 %all_gather.3 = bf16[1024,128]{1,0:T(8,128)(2,1)S(1)} all-gather(bf16[128,128]{1,0:T(8,128)(2,1)} %param.13), channel_id=1, replica_groups=mesh['grp'=4,'dev'=8] {'dev'}, dimensions={0}, use_global_device_ids=true | all-gather | bytes 294912 | tf_op jit(solution)/shard_map/all_gather | solution.py:45
  45.6 0.7 collective-permute-start.1
  46.4 3.5 %collective-permute-done.1 = bf16[128,64]{1,0:T(8,128)(2,1)S(1)} collective-permute-done((bf16[128,64]{1,0:T(8,128)(2,1)S(1)}, bf16[128,64]{1,0:T(8,128)(2,1)S(1)}, u32[]{:S(2)}, u32[]{:S(2)}) %collective-permute-start.1) | collective-permute-done | bytes 16416 | tf_op jit(solution)/shard_map/ppermute | solution.py:16
  49.9 3.1 %collective-permute-start.2 = (bf16[128,64]{1,0:T(8,128)(2,1)S(1)}, bf16[128,64]{1,0:T(8,128)(2,1)S(1)}, u32[]{:S(2)}, u32[]{:S(2)}) collective-permute-start(bf16[128,64]{1,0:T(8,128)(2,1)S(1)} %collective-permute-done.1), channel_id=1, source_target_pairs={{0,7},{1,0},{2,1},{3,2},{4,3},{5,4},{6,5},{7,6},{8,15},{9,8},{10,9... | collective-permute-start | bytes 49160 | tf_op jit(solution)/shard_map/ppermute | solution.py:16
  53.0 1.6 collective-permute-done.2
  54.6 5.0 %collective-permute-start.3 = (bf16[128,64]{1,0:T(8,128)(2,1)S(1)}, bf16[128,64]{1,0:T(8,128)(2,1)S(1)}, u32[]{:S(2)}, u32[]{:S(2)}) collective-permute-start(bf16[128,64]{1,0:T(8,128)(2,1)S(1)} %collective-permute-done.2), channel_id=1, source_target_pairs={{0,7},{1,0},{2,1},{3,2},{4,3},{5,4},{6,5},{7,6},{8,15},{9,8},{10,9... | collective-permute-start | bytes 49160 | tf_op jit(solution)/shard_map/ppermute | solution.py:16
  59.6 1.6 collective-permute-done.3
  61.2 5.0 %collective-permute-start.4 = (bf16[128,64]{1,0:T(8,128)(2,1)S(1)}, bf16[128,64]{1,0:T(8,128)(2,1)S(1)}, u32[]{:S(2)}, u32[]{:S(2)}) collective-permute-start(bf16[128,64]{1,0:T(8,128)(2,1)S(1)} %collective-permute-done.3), channel_id=1, source_target_pairs={{0,7},{1,0},{2,1},{3,2},{4,3},{5,4},{6,5},{7,6},{8,15},{9,8},{10,9... | collective-permute-start | bytes 49160 | tf_op jit(solution)/shard_map/ppermute | solution.py:16
  66.2 1.6 collective-permute-done.4
  67.8 5.0 %collective-permute-start.5 = (bf16[128,64]{1,0:T(8,128)(2,1)S(1)}, bf16[128,64]{1,0:T(8,128)(2,1)S(1)}, u32[]{:S(2)}, u32[]{:S(2)}) collective-permute-start(bf16[128,64]{1,0:T(8,128)(2,1)S(1)} %collective-permute-done.4), channel_id=1, source_target_pairs={{0,7},{1,0},{2,1},{3,2},{4,3},{5,4},{6,5},{7,6},{8,15},{9,8},{10,9... | collective-permute-start | bytes 49160 | tf_op jit(solution)/shard_map/ppermute | solution.py:16
  72.8 1.6 collective-permute-done.5
  74.4 5.0 %collective-permute-start.6 = (bf16[128,64]{1,0:T(8,128)(2,1)S(1)}, bf16[128,64]{1,0:T(8,128)(2,1)S(1)}, u32[]{:S(2)}, u32[]{:S(2)}) collective-permute-start(bf16[128,64]{1,0:T(8,128)(2,1)S(1)} %collective-permute-done.5), channel_id=1, source_target_pairs={{0,7},{1,0},{2,1},{3,2},{4,3},{5,4},{6,5},{7,6},{8,15},{9,8},{10,9... | collective-permute-start | bytes 49160 | tf_op jit(solution)/shard_map/ppermute | solution.py:16
  79.5 1.6 collective-permute-done.6
  81.2 4.5 %while.32 = (s32[]{:T(128)}, f32[2,512,64]{1,0,2:T(2,128)S(1)}, f32[2,512]{1,0:T(2,128)S(1)}, f32[1024]{0:T(1024)S(1)}, bf16[2,512,128]{2,1,0:T(8,128)(2,1)S(1)}...) while((s32[]{:T(128)}, f32[2,512,64]{1,0,2:T(2,128)S(1)}, ...), condition=%wide.region_3.4_spmd, body=%wide.region_2.3_spmd.sunk | while | flops 203948032 | bytes 1321065 | solution.py:55
  81.2 0.9 fusion.81
  82.2 1.2 dynamic_update_slice.5
  83.5 0.9 fusion.81
  84.5 1.2 dynamic_update_slice.5
  85.8 0.8 copy.22
  86.8 33.9 %all-reduce.2.cloned.1.call-done = f32[1024,64]{0,1:T(8,128)} async-done(((f32[1024,64]{0,1:T(8,128)}), f32[1024,64]{0,1:T(8,128)}) %all-reduce.2.cloned.1.call-update) | async-done | bytes 262160 | tf_op jit(solution)/shard_map/psum | solution.py:56
  120.7 1.0 subtract_convert_fusion
  121.9 1.8 while.33
  121.9 0.9 fusion.85
  122.8 0.9 fusion.85
  124.4 1.3 while.34
  126.0 40.1 %psum.15 = f32[160,64]{1,0:T(8,128)S(1)} all-reduce(f32[160,64]{1,0:T(8,128)S(1)} %convolution_bitcast_fusion.1), channel_id=1, replica_groups=mesh['grp'=4,'dev'=8] {'grp','dev'}, use_global_device_ids=true, to_apply=%region_11.12 | all-reduce | flops 10240 | bytes 81920 | tf_op jit(solution)/shard_map/psum | solution.py:88
  166.1 1.0 convolution_bitcast_fusion
  167.1 20.0 %reduce-scatter.2.cloned.1.call-done = f32[128,64]{0,1:T(8,128)} async-done(((f32[1024,64]{0,1:T(8,128)}), f32[128,64]{0,1:T(8,128)}) %reduce-scatter.2.cloned.1.call-update) | async-done | bytes 32784 | tf_op jit(solution)/shard_map/reduce_scatter | solution.py:71
  187.1 1.4 broadcast_multiply_fusion
  188.5 0.7 copy.60
  (55 shorter events, 3.6 us)
Async XLA Ops:
  7.2 118.6 %copy-start = (bf16[512,160]{0,1:T(8,128)(2,1)S(1)}, bf16[512,160]{0,1:T(8,128)(2,1)}, u32[]{:S(2)}) copy-start(bf16[512,160]{0,1:T(8,128)(2,1)} %param.18) | copy-start | bytes 491524
  7.2 38.2 %copy-start.2 = (bf16[1024,128]{1,0:T(8,128)(2,1)S(1)}, bf16[1024,128]{1,0:T(8,128)(2,1)}, u32[]{:S(2)}) copy-start(bf16[1024,128]{1,0:T(8,128)(2,1)} %param.15) | copy-start | bytes 786436
  7.2 113.5 %all-reduce.2.cloned.1.call-start = ((), (), s32[]{:S(2)}) async-start(), calls=%async_computation.1 | async-start | bytes 524288 | tf_op jit(solution)/shard_map/psum | solution.py:56
  8.1 37.5 %collective-permute-start = (bf16[128,64]{1,0:T(8,128)(2,1)S(1)}, bf16[128,64]{1,0:T(8,128)(2,1)S(1)}, u32[]{:S(2)}, u32[]{:S(2)}) collective-permute-start(bf16[128,64]{1,0:T(8,128)(2,1)S(1)} %copy.11), channel_id=1, source_target_pairs={{0,7},{1,0},{2,1},{3,2},{4,3},{5,4},{6,5},{7,6},{8,15},{9,8},{10,9... | collective-permute-start | bytes 49160 | tf_op jit(solution)/shard_map/ppermute | solution.py:16
  45.6 4.3 %collective-permute-start.1 = (bf16[128,64]{1,0:T(8,128)(2,1)S(1)}, bf16[128,64]{1,0:T(8,128)(2,1)S(1)}, u32[]{:S(2)}, u32[]{:S(2)}) collective-permute-start(bf16[128,64]{1,0:T(8,128)(2,1)S(1)} %collective-permute-done), channel_id=1, source_target_pairs={{0,7},{1,0},{2,1},{3,2},{4,3},{5,4},{6,5},{7,6},{8,15},{9,8},{10,9... | collective-permute-start | bytes 49160 | tf_op jit(solution)/shard_map/ppermute | solution.py:16
  49.9 4.7 %collective-permute-start.2 = (bf16[128,64]{1,0:T(8,128)(2,1)S(1)}, bf16[128,64]{1,0:T(8,128)(2,1)S(1)}, u32[]{:S(2)}, u32[]{:S(2)}) collective-permute-start(bf16[128,64]{1,0:T(8,128)(2,1)S(1)} %collective-permute-done.1), channel_id=1, source_target_pairs={{0,7},{1,0},{2,1},{3,2},{4,3},{5,4},{6,5},{7,6},{8,15},{9,8},{10,9... | collective-permute-start | bytes 49160 | tf_op jit(solution)/shard_map/ppermute | solution.py:16
  54.6 6.6 %collective-permute-start.3 = (bf16[128,64]{1,0:T(8,128)(2,1)S(1)}, bf16[128,64]{1,0:T(8,128)(2,1)S(1)}, u32[]{:S(2)}, u32[]{:S(2)}) collective-permute-start(bf16[128,64]{1,0:T(8,128)(2,1)S(1)} %collective-permute-done.2), channel_id=1, source_target_pairs={{0,7},{1,0},{2,1},{3,2},{4,3},{5,4},{6,5},{7,6},{8,15},{9,8},{10,9... | collective-permute-start | bytes 49160 | tf_op jit(solution)/shard_map/ppermute | solution.py:16
  61.2 6.6 %collective-permute-start.4 = (bf16[128,64]{1,0:T(8,128)(2,1)S(1)}, bf16[128,64]{1,0:T(8,128)(2,1)S(1)}, u32[]{:S(2)}, u32[]{:S(2)}) collective-permute-start(bf16[128,64]{1,0:T(8,128)(2,1)S(1)} %collective-permute-done.3), channel_id=1, source_target_pairs={{0,7},{1,0},{2,1},{3,2},{4,3},{5,4},{6,5},{7,6},{8,15},{9,8},{10,9... | collective-permute-start | bytes 49160 | tf_op jit(solution)/shard_map/ppermute | solution.py:16
  67.8 6.6 %collective-permute-start.5 = (bf16[128,64]{1,0:T(8,128)(2,1)S(1)}, bf16[128,64]{1,0:T(8,128)(2,1)S(1)}, u32[]{:S(2)}, u32[]{:S(2)}) collective-permute-start(bf16[128,64]{1,0:T(8,128)(2,1)S(1)} %collective-permute-done.4), channel_id=1, source_target_pairs={{0,7},{1,0},{2,1},{3,2},{4,3},{5,4},{6,5},{7,6},{8,15},{9,8},{10,9... | collective-permute-start | bytes 49160 | tf_op jit(solution)/shard_map/ppermute | solution.py:16
  74.4 6.6 %collective-permute-start.6 = (bf16[128,64]{1,0:T(8,128)(2,1)S(1)}, bf16[128,64]{1,0:T(8,128)(2,1)S(1)}, u32[]{:S(2)}, u32[]{:S(2)}) collective-permute-start(bf16[128,64]{1,0:T(8,128)(2,1)S(1)} %collective-permute-done.5), channel_id=1, source_target_pairs={{0,7},{1,0},{2,1},{3,2},{4,3},{5,4},{6,5},{7,6},{8,15},{9,8},{10,9... | collective-permute-start | bytes 49160 | tf_op jit(solution)/shard_map/ppermute | solution.py:16
  85.7 0.9 copy-start.4
  85.7 35.0 %copy-start.5 = (bf16[1024,64]{0,1:T(8,128)(2,1)S(1)}, bf16[1024,64]{0,1:T(8,128)(2,1)}, u32[]{:S(2)}) copy-start(bf16[1024,64]{0,1:T(8,128)(2,1)} %param.16) | copy-start | bytes 393220
  86.5 100.6 %reduce-scatter.2.cloned.1.call-start = ((), (), s32[]{:S(2)}) async-start(), calls=%async_computation.2 | async-start | bytes 294912 | tf_op jit(solution)/shard_map/reduce_scatter | solution.py:71
  123.7 0.7 copy-start.3
  125.7 40.4 %copy-start.6 = (f32[160]{0:T(256)S(1)}, f32[160]{0:T(256)}, u32[]{:S(2)}) copy-start(f32[160]{0:T(256)} %param.19) | copy-start | bytes 1924
  125.7 62.7 %copy-start.1 = (f32[1024,64]{0,1:T(8,128)S(1)}, f32[1024,64]{0,1:T(8,128)}, u32[]{:S(2)}) copy-start(f32[1024,64]{0,1:T(8,128)} %all-reduce.2.cloned.1.call-done) | copy-start | bytes 786436
Sparse Core Ops, SparseCore 0:
  86.7 34.0 all-reduce.1
  124.6 62.4 reduce-scatter.1
